TPU v7x, 256 devices: a whole 4x4x8 slice. The times are simulated.
256 devices in a mesh: wide: 32 (over x, z), blk: 8 (over y, core).
Axes of the slice: x: 4, y: 4, z: 8, core: 2. Of those that a mesh axis runs over, the one named last changes fastest.
Arguments:
- amplitudes: bfloat16 [32, 32, 32, 4096], P('blk', 'wide'), may hold values from -6 to 6
- integrals: bfloat16 [32, 2, 2048, 4096], P('wide', None, 'blk'), may hold values from -0.09375 to 0.09375
- owner: int32 [32], replicated, may hold values from 0 to 31, each once
- targets: int32 [32, 2], replicated, may hold values from 0 to 31, all different within a row
- counts: int32 [32], replicated, may hold values from 1 to 2, 48 in all
Outputs:
- ladder: bfloat16 [32, 32, 32, 2048], P(None, 'blk', 'wide')
Inputs may be any that keep to these rules, and one draw needn't show every extreme that they name: Each contracted tile has its own owner slot. `targets`: the output tiles of one contracted tile are distinct, and every output tile is named by some contracted tile. The counts sum to 48 and one of them is 2.
All inputs are finite; a program needn't handle non-finite values.
Results may differ from a plain program's by a relative error of at most 0.0044.
Values may be sent and summed in bfloat16 or wider, within the bound.
A program may use at most 128 MiB of HBM per device.

v0:
```python
import jax
import jax.numpy as jnp
from jax import lax
from jax.sharding import PartitionSpec as P


def body(amplitudes, integrals, owner, targets, counts):
    wide_count = lax.axis_size("wide")
    my_index = lax.axis_index("wide")
    tile_ids = jnp.arange(owner.shape[0], dtype=jnp.int32)
    holder = jnp.sum(jnp.where(owner[None, :] == tile_ids[:, None], tile_ids[None, :], 0), axis=1)
    ordered = jnp.take(amplitudes, holder, axis=2)
    my_tile = lax.all_to_all(ordered, "wide", split_axis=2, concat_axis=1, tiled=True)
    my_holder = lax.dynamic_index_in_dim(holder, my_index, 0, keepdims=False)
    my_count = lax.dynamic_index_in_dim(counts, my_holder, 0, keepdims=False)
    slot_ids = jnp.arange(targets.shape[1], dtype=jnp.int32)
    live_slots = (slot_ids < my_count).astype(jnp.float32)
    my_integrals = integrals[0]
    width = my_tile.shape[3]
    pair_rows = my_tile.reshape(-1, width)
    partial_value = jnp.einsum(
        "rc,kac->rka",
        pair_rows,
        lax.all_gather(my_integrals, "blk", axis=1, tiled=True),
        preferred_element_type=jnp.float32,
    )
    shaped = (partial_value * live_slots[None, :, None]).astype(jnp.bfloat16)
    shaped = shaped.reshape(my_tile.shape[0], my_tile.shape[1], targets.shape[1], shaped.shape[2])
    received = lax.all_to_all(shaped, "wide", split_axis=1, concat_axis=2, tiled=True)
    slot_targets = jnp.take(targets, holder, axis=0).reshape(-1)
    window_ids = jnp.arange(wide_count, dtype=jnp.int32)
    selector = (slot_targets[None, :] == window_ids[:, None]).astype(jnp.bfloat16)
    ladder = jnp.einsum("ps,ijsa->pija", selector, received, preferred_element_type=jnp.float32)
    return ladder.astype(jnp.bfloat16)


def solution(mesh):
    placed = (P("blk", "wide", None, None), P("wide", None, "blk", None), P(), P(), P())
    return jax.shard_map(
        body, mesh=mesh, in_specs=placed, out_specs=P(None, "blk", "wide", None), check_vma=False
    )
```

profile of v0, /device:TPU:8, one launch (start us, length us, event | category | flops | bytes accessed | tf_op | source)
XLA Modules:
  0.0 236.6 jit_solution(17188635275053602947)
XLA Ops:
  6.5 0.0 copy-start
  6.5 0.0 all-gather.3.cloned.1.call-start
  6.5 0.7 all-gather.3.cloned.1.call-update
  7.3 2.0 copy.32
  9.3 0.8 select_reduce_fusion
  10.1 1.4 gather_fusion.1
  11.6 1.5 fusion.9
  13.1 11.3 %all-to-all-start = ((bf16[4,1,32,4096]{3,0,1,2:T(4,128)(2,1)}), bf16[4,1,32,4096]{3,0,1,2:T(4,128)(2,1)S(1)}, u32[]{:S(2)}, u32[]{:S(2)}) async-start(bf16[4,1,32,4096]{3,0,1,2:T(4,128)(2,1)} %fusion.9), calls=%async_computation | async-start | bytes 2097152 | tf_op jit(solution)/shard_map/all_to_all | solution.py:13
  24.4 0.6 dynamic_slice.7
  27.0 1.3 dynamic_slice.8
  28.2 0.7 compare_convert_fusion
  28.9 24.1 %all-to-all-done = bf16[4,1,32,4096]{3,0,1,2:T(4,128)(2,1)S(1)} async-done(((bf16[4,1,32,4096]{3,0,1,2:T(4,128)(2,1)}), bf16[4,1,32,4096]{3,0,1,2:T(4,128)(2,1)S(1)}, u32[]{:S(2)}, u32[]{:S(2)}) %all-to-all-start) | async-done | bytes 1048608 | tf_op jit(solution)/shard_map/all_to_all | solution.py:13
  53.0 0.6 copy.24
  53.6 116.9 %all-gather.3.cloned.1.call-done = bf16[1,2,2048,4096]{3,2,1,0:T(8,128)(2,1)} async-done(((bf16[1,2,256,4096]{3,2,1,0:T(8,128)(2,1)}), bf16[1,2,2048,4096]{3,2,1,0:T(8,128)(2,1)}) %all-gather.3.cloned.1.call-update) | async-done | bytes 33554448 | tf_op jit(solution)/shard_map/all_gather | solution.py:24
  170.5 16.0 %fusion.5 = bf16[128,2,2048]{2,0,1:T(8,128)(2,1)S(1)} fusion(bf16[128,4096,1]{1,0,2:T(8,128)(2,1)S(1)} %bitcast.36, bf16[1,2,2048,4096]{3,2,1,0:T(8,128)(2,1)} %all-gather.3.cloned.1.call-done, f32[2]{0:T(128)S(1)} %compare_convert_fusion), kind=kOutput, calls=%fused_computation.6 | convolution fusion | flops 4296015872 | bytes 35651592 | tf_op jit(solution)/shard_map/rc,kac->rka/dot_general | solution.py:21
  186.6 1.8 copy.25
  188.3 9.8 %all-to-all-start.1 = ((bf16[4,32,2,2048]{3,0,2,1:T(4,128)(2,1)}), bf16[4,32,2,2048]{3,0,2,1:T(4,128)(2,1)S(1)}, u32[]{:S(2)}, u32[]{:S(2)}) async-start(bf16[4,32,2,2048]{3,0,2,1:T(4,128)(2,1)} %copy.25), calls=%async_computation.1 | async-start | bytes 2097152 | tf_op jit(solution)/shard_map/all_to_all | solution.py:29
  198.2 0.0 copy-done
  198.2 0.1 copy.21
  198.3 0.6 gather_fusion
  198.9 0.1 broadcast_select_fusion
  198.9 0.1 select_n.56
  199.0 28.2 %all-to-all-done.1 = bf16[4,32,2,2048]{3,0,2,1:T(4,128)(2,1)S(1)} async-done(((bf16[4,32,2,2048]{3,0,2,1:T(4,128)(2,1)}), bf16[4,32,2,2048]{3,0,2,1:T(4,128)(2,1)S(1)}, u32[]{:S(2)}, u32[]{:S(2)}) %all-to-all-start.1) | async-done | bytes 1048608 | tf_op jit(solution)/shard_map/all_to_all | solution.py:29
  227.2 1.3 fusion.8
  228.5 1.2 copy.27
  (3 shorter events, 0.0 us)
Async XLA Ops:
  6.5 191.7 %copy-start = (s32[32,2]{0,1:T(2,128)S(1)}, s32[32,2]{0,1:T(2,128)}, u32[]{:S(2)}) copy-start(s32[32,2]{0,1:T(2,128)} %param.8) | copy-start | bytes 772
  6.5 164.0 %all-gather.3.cloned.1.call-start = ((), (), s32[]{:S(2)}) async-start(), calls=%async_computation.2 | async-start | bytes 37748736 | tf_op jit(solution)/shard_map/all_gather | solution.py:24
  13.1 39.9 %all-to-all-start = ((bf16[4,1,32,4096]{3,0,1,2:T(4,128)(2,1)}), bf16[4,1,32,4096]{3,0,1,2:T(4,128)(2,1)S(1)}, u32[]{:S(2)}, u32[]{:S(2)}) async-start(bf16[4,1,32,4096]{3,0,1,2:T(4,128)(2,1)} %fusion.9), calls=%async_computation | async-start | bytes 2097152 | tf_op jit(solution)/shard_map/all_to_all | solution.py:13
  188.3 38.9 %all-to-all-start.1 = ((bf16[4,32,2,2048]{3,0,2,1:T(4,128)(2,1)}), bf16[4,32,2,2048]{3,0,2,1:T(4,128)(2,1)S(1)}, u32[]{:S(2)}, u32[]{:S(2)}) async-start(bf16[4,32,2,2048]{3,0,2,1:T(4,128)(2,1)} %copy.25), calls=%async_computation.1 | async-start | bytes 2097152 | tf_op jit(solution)/shard_map/all_to_all | solution.py:29
Sparse Core Ops, SparseCore 0:
  9.2 161.2 all-gather.2
where the time goes:
time: 237 us
  waiting for transfers between devices  170 us (72%)
  starting transfers between devices  21.2 us (9%)
  matrix products  17.3 us (7%)
  between operations  15.4 us (6%)
  local copies, waits for them, and re-layouts  9.66 us (4%)
  other arithmetic  3.06 us (1%)
    all_gather x1, waiting for transfers between devices, body(): lax.all_gather(my_integrals, 'blk', axis=1, tiled=True)  117 us
    all_to_all x1, waiting for transfers between devices, body(): lax.all_to_all(shaped, 'wide', split_axis=1, concat_axis=2, tiled=True)  28.2 us
    all_to_all x1, waiting for transfers between devices, body(): lax.all_to_all(ordered, 'wide', split_axis=2, concat_axis=1, tiled=True)  24.1 us
    dot_general x1, matrix products, body(): jnp.einsum('rc,kac->rka', pair_rows, lax.all_gather(my_integrals, 'blk',...  16 us
    all_to_all x1, starting transfers between devices, body(): lax.all_to_all(ordered, 'wide', split_axis=2, concat_axis=1, tiled=True)  11.3 us
    all_to_all x1, starting transfers between devices, body(): lax.all_to_all(shaped, 'wide', split_axis=1, concat_axis=2, tiled=True)  9.84 us
  transfers between devices with their start and end apart: 3, of which 3 were waited for; matrix products, arithmetic and copies ran while one was open for 4% of the time, Pallas kernels for 0%

commit v1 on v0

--- a/solution.py
+++ b/solution.py
@@ -18,10 +18,16 @@
     my_integrals = integrals[0]
     width = my_tile.shape[3]
     pair_rows = my_tile.reshape(-1, width)
+    _extend_domain = lambda own_rows, axis_name: jnp.concatenate(
+        lax.all_to_all(
+            jnp.stack([own_rows for _ in range(lax.axis_size(axis_name))]), axis_name, 0, 0
+        ),
+        1,
+    )
     partial_value = jnp.einsum(
         "rc,kac->rka",
         pair_rows,
-        lax.all_gather(my_integrals, "blk", axis=1, tiled=True),
+        _extend_domain(my_integrals, "blk"),
         preferred_element_type=jnp.float32,
     )
     shaped = (partial_value * live_slots[None, :, None]).astype(jnp.bfloat16)

time: 237 us -> 505 us (2.13)
  waiting for transfers between devices: 170 us -> 386 us
  blocking collectives: 0 us -> 39.7 us
  local copies, waits for them, and re-layouts: 9.66 us -> 44.3 us
  between operations: 15.4 us -> 2.04 us
  starting transfers between devices: 21.2 us -> 12.6 us
    all_to_all x1, waiting for transfers between devices: 24.1 us -> 359 us  [body(): lax.all_to_all(jnp.stack([own_rows for _ in range(lax.axis_size(axis_name...]
    all_gather x1 -> x0, waiting for transfers between devices: 117 us -> none  [body(): lax.all_gather(my_integrals, 'blk', axis=1, tiled=True)]
    all_to_all x0 -> x1, blocking collectives: none -> 39.7 us  [body(): lax.all_to_all(ordered, 'wide', split_axis=2, concat_axis=1, tiled=True)]
    reshape x0 -> x1, local copies, waits for them, and re-layouts: none -> 22.9 us  [body(): jnp.concatenate(lax.all_to_all(jnp.stack([own_rows for _ in range(lax.axi...]
    another operation x0 -> x1, local copies, waits for them, and re-layouts: none -> 12.4 us  [body(): jnp.stack([own_rows for _ in range(lax.axis_size(axis_name))])]
  transfers between devices with their start and end apart: 3 -> 2, of which waited for: 3 -> 2; matrix products, arithmetic and copies ran while one was open for 4% -> 1% of each run, Pallas kernels for 0% -> 0%
where the time goes in v1:
time: 505 us; the launch traced here: 504 us
  waiting for transfers between devices  386 us (76%)
  local copies, waits for them, and re-layouts  44.3 us (9%)
  blocking collectives  39.7 us (8%)
  matrix products  17.4 us (3%)
  starting transfers between devices  12.6 us (2%)
    all_to_all x1, waiting for transfers between devices, body(): lax.all_to_all(jnp.stack([own_rows for _ in range(lax.axis_size(axis_name...  359 us
    all_to_all x1, blocking collectives, body(): lax.all_to_all(ordered, 'wide', split_axis=2, concat_axis=1, tiled=True)  39.7 us
    all_to_all x1, waiting for transfers between devices, body(): lax.all_to_all(shaped, 'wide', split_axis=1, concat_axis=2, tiled=True)  27.6 us
    reshape x1, local copies, waits for them, and re-layouts, body(): jnp.concatenate(lax.all_to_all(jnp.stack([own_rows for _ in range(lax.axi...  22.9 us
    dot_general x1, matrix products, body(): jnp.einsum('rc,kac->rka', pair_rows, _extend_domain(my_integrals, 'blk'),...  16.1 us
    another operation x1, local copies, waits for them, and re-layouts, body(): jnp.stack([own_rows for _ in range(lax.axis_size(axis_name))])  12.4 us
  transfers between devices with their start and end apart: 2, of which 2 were waited for; matrix products, arithmetic and copies ran while one was open for 1% of the time, Pallas kernels for 0%

profile of v1, /device:TPU:8, one launch (start us, length us, event | category | flops | bytes accessed | tf_op | source)
XLA Modules:
  0.0 504.3 jit_solution(6126716716485154112)
XLA Ops:
  0.0 0.8 select_reduce_fusion
  0.8 2.0 copy.34
  2.8 1.4 gather_fusion.1
  4.3 0.6 fusion.2
  4.9 39.7 %all_to_all.23 = bf16[4,1,32,4096]{3,0,1,2:T(4,128)(2,1)S(1)} all-to-all(bf16[4,1,32,4096]{3,0,1,2:T(4,128)(2,1)S(1)} %fusion.2), channel_id=1, replica_groups=mesh['wide'=32,'blk'=8] {'wide'}, dimensions={2} | all-to-all | bytes 2097152 | tf_op jit(solution)/shard_map/all_to_all | solution.py:13
  44.6 12.4 %stack.3 = bf16[8,2,256,4096]{3,2,1,0:T(8,128)(2,1)} broadcast(bf16[2,256,4096]{2,1,0:T(8,128)(2,1)} %bitcast.35), dimensions={1,2,3} | broadcast | bytes 37748736 | tf_op jit(solution)/shard_map/stack | solution.py:23
  57.0 0.0 copy-start.1
  57.0 7.5 %all-to-all-start.1 = ((bf16[8,2,256,4096]{3,2,1,0:T(8,128)(2,1)}), bf16[8,2,256,4096]{3,2,1,0:T(8,128)(2,1)}, u32[]{:S(2)}, u32[]{:S(2)}) async-start(bf16[8,2,256,4096]{3,2,1,0:T(8,128)(2,1)} %stack.3), calls=%async_computation.1 | async-start | bytes 67108864 | tf_op jit(solution)/shard_map/all_to_all | solution.py:22
  64.5 0.6 dynamic_slice.7
  67.1 0.0 copy-done.1
  67.1 0.6 dynamic_slice.8
  67.7 0.6 compare_convert_fusion
  68.3 0.6 copy.25
  68.9 358.5 %all-to-all-done.1 = bf16[8,2,256,4096]{3,2,1,0:T(8,128)(2,1)} async-done(((bf16[8,2,256,4096]{3,2,1,0:T(8,128)(2,1)}), bf16[8,2,256,4096]{3,2,1,0:T(8,128)(2,1)}, u32[]{:S(2)}, u32[]{:S(2)}) %all-to-all-start.1) | async-done | bytes 33554464 | tf_op jit(solution)/shard_map/all_to_all | solution.py:22
  427.5 22.9 %copy.26 = bf16[2,8,256,4096]{3,2,1,0:T(8,128)(2,1)} copy(bf16[2,8,256,4096]{3,2,0,1:T(8,128)(2,1)} %bitcast.10) | data formatting | bytes 67108864 | tf_op jit(solution)/shard_map/reshape | solution.py:21
  450.4 0.0 copy-start
  450.4 16.1 %fusion = bf16[128,2,2048]{2,0,1:T(8,128)(2,1)S(1)} fusion(bf16[128,4096,1]{1,0,2:T(8,128)(2,1)S(1)} %bitcast.34, bf16[2,2048,4096]{2,1,0:T(8,128)(2,1)} %bitcast.32, f32[2]{0:T(128)S(1)} %compare_convert_fusion), kind=kOutput, calls=%fused_computation.3 | convolution fusion | flops 4296015872 | bytes 35651592 | tf_op jit(solution)/shard_map/rc,kac->rka/dot_general | solution.py:27
  466.4 1.8 copy.27
  468.2 5.1 %all-to-all-start.2 = ((bf16[4,32,2,2048]{3,0,2,1:T(4,128)(2,1)}), bf16[4,32,2,2048]{3,0,2,1:T(4,128)(2,1)S(1)}, u32[]{:S(2)}, u32[]{:S(2)}) async-start(bf16[4,32,2,2048]{3,0,2,1:T(4,128)(2,1)} %copy.27), calls=%async_computation.2 | async-start | bytes 2097152 | tf_op jit(solution)/shard_map/all_to_all | solution.py:35
  473.3 0.0 copy-done
  473.3 0.1 copy.22
  473.4 0.6 gather_fusion
  474.0 0.1 broadcast_select_fusion
  474.1 0.1 select_n.56
  474.2 27.6 %all-to-all-done.2 = bf16[4,32,2,2048]{3,0,2,1:T(4,128)(2,1)S(1)} async-done(((bf16[4,32,2,2048]{3,0,2,1:T(4,128)(2,1)}), bf16[4,32,2,2048]{3,0,2,1:T(4,128)(2,1)S(1)}, u32[]{:S(2)}, u32[]{:S(2)}) %all-to-all-start.2) | async-done | bytes 1048608 | tf_op jit(solution)/shard_map/all_to_all | solution.py:35
  501.8 1.3 fusion.1
  503.1 1.2 copy.29
  (3 shorter events, 0.0 us)
Async XLA Ops:
  57.0 10.1 %copy-start.1 = (s32[32]{0:T(128)S(1)}, s32[32]{0:T(128)}, u32[]{:S(2)}) copy-start(s32[32]{0:T(128)} %param.9) | copy-start | bytes 388
  57.0 370.5 %all-to-all-start.1 = ((bf16[8,2,256,4096]{3,2,1,0:T(8,128)(2,1)}), bf16[8,2,256,4096]{3,2,1,0:T(8,128)(2,1)}, u32[]{:S(2)}, u32[]{:S(2)}) async-start(bf16[8,2,256,4096]{3,2,1,0:T(8,128)(2,1)} %stack.3), calls=%async_computation.1 | async-start | bytes 67108864 | tf_op jit(solution)/shard_map/all_to_all | solution.py:22
  450.4 23.0 %copy-start = (s32[32,2]{0,1:T(2,128)S(1)}, s32[32,2]{0,1:T(2,128)}, u32[]{:S(2)}) copy-start(s32[32,2]{0,1:T(2,128)} %param.8) | copy-start | bytes 772
  468.2 33.6 %all-to-all-start.2 = ((bf16[4,32,2,2048]{3,0,2,1:T(4,128)(2,1)}), bf16[4,32,2,2048]{3,0,2,1:T(4,128)(2,1)S(1)}, u32[]{:S(2)}, u32[]{:S(2)}) async-start(bf16[4,32,2,2048]{3,0,2,1:T(4,128)(2,1)} %copy.27), calls=%async_computation.2 | async-start | bytes 2097152 | tf_op jit(solution)/shard_map/all_to_all | solution.py:35
